TPU v7x, 256 devices: a whole 4x4x8 slice. The times are simulated.
256 devices in a mesh: gx: 4 (over y), gy: 8 (over z_hi, core), gz: 8 (over z_lo, x).
Axes of the slice: x: 4, y: 4, z: 8 (z_hi: 4, z_lo: 2; z = z_hi * 2 + z_lo), core: 2. Of those that a mesh axis runs over, the one named last changes fastest.
Arguments:
- interior_inverse: bfloat16 [2048, 512, 512], P(('gx', 'gy', 'gz')), may hold values from -0.25 to 0.25
- interior_to_face: bfloat16 [2048, 512, 384], P(('gx', 'gy', 'gz')), may hold values from -0.25 to 0.25
- face_to_interior: bfloat16 [2048, 384, 512], P(('gx', 'gy', 'gz')), may hold values from -6 to 6
- face_diag: bfloat16 [2048, 6, 4096], P(('gx', 'gy', 'gz')), may hold values from -6 to 6
- element_cell: int32 [2048], P(('gx', 'gy', 'gz')), may hold values from 0 to 7, as said below
- face_orient: int32 [2048, 6], P(('gx', 'gy', 'gz')), may hold values from 0 to 7
- face_owner: int32 [8, 16, 16, 3], P('gx', 'gy', 'gz'), may hold values from 0 to 23, as said below
- prescribed_face_mask: int32 [8, 16, 16, 3], P('gx', 'gy', 'gz'), may hold values 0 or 1
Outputs:
- trace_rows: bfloat16 [4, 8, 192, 11, 4096], P('gx', 'gy', 'gz')
Inputs may be any that keep to these rules, and one draw needn't show every extreme that they name: `element_cell`: on each device the 8 entries are a permutation of 0 to 7. `face_owner`: within each device's block of 2 x 2 x 2 x 3 entries every value of 0 to 23 appears once.
All inputs are finite; a program needn't handle non-finite values. No bound on the sum of `prescribed_face_mask` on one device may be relied on, other than what follows from the above.
Results may differ from a plain program's by a relative error of at most 0.0052.
Values may be sent and summed in bfloat16 or wider, within the bound.
A program may use at most 128 MiB of HBM per device.

v0:
```python
import jax
import jax.numpy as jnp
from jax import lax
from jax.sharding import PartitionSpec as P

Q = 8
NFACE = 64
EX = 2
EY = 2
ELEMENTS_Z_PART = 2
F_DEV = 24


def shifted(value, axis, steps):
    count = lax.axis_size(axis)
    pairs = [(source, (source + steps) % count) for source in range(count)]
    return lax.ppermute(value, axis, pairs)


def orientation_map(codes):
    nodes = jnp.arange(NFACE, dtype=jnp.int32)
    first = nodes // Q
    second = nodes % Q
    codes = codes[..., None]
    swapped = codes // 4 % 2 == 1
    new_first = jnp.where(swapped, second, first)
    new_second = jnp.where(swapped, first, second)
    new_first = jnp.where(codes % 2 == 1, Q - 1 - new_first, new_first)
    new_second = jnp.where(codes // 2 % 2 == 1, Q - 1 - new_second, new_second)
    return Q * new_first + new_second


def identity_row():
    first = jnp.eye(NFACE, dtype=jnp.float32).reshape(1, NFACE * NFACE)
    rest = jnp.zeros((10, NFACE * NFACE), jnp.float32)
    return jnp.concatenate([first, rest], axis=0).astype(jnp.bfloat16)


def assemble(left_all, right_all, direction, flags):
    upper = 2 * direction + 1
    lower = 2 * direction
    diagonal = (
        left_all[:, :, :, upper].astype(jnp.float32) + right_all[:, :, :, lower].astype(jnp.float32)
    ).astype(jnp.bfloat16)
    row = jnp.concatenate(
        [
            diagonal[:, :, :, None],
            left_all[:, :, :, :upper],
            left_all[:, :, :, upper + 1 :],
            right_all[:, :, :, :lower],
            right_all[:, :, :, lower + 1 :],
        ],
        axis=3,
    )
    marked = flags[:, :, :, direction][:, :, :, None, None] == 1
    return jnp.where(marked, identity_row()[None, None, None], row)


def upper_neighbours(element_lattice, direction):
    lower_rows = element_lattice[:, :, :, 2 * direction]
    extent = lower_rows.shape[direction]
    rim_rows = lax.slice_in_dim(lower_rows, 0, 1, axis=direction)
    if direction == 0:
        arrived = shifted(rim_rows, "gx", -1)
    elif direction == 1:
        arrived = shifted(rim_rows, "gy", -1)
    else:
        arrived = shifted(rim_rows, "gz", -1)
    inner_rows = lax.slice_in_dim(lower_rows, 1, extent, axis=direction)
    return jnp.concatenate([inner_rows, arrived], axis=direction)


def shards(
    interior_inverse,
    interior_to_face,
    face_to_interior,
    face_diag,
    element_cell,
    face_orient,
    face_owner,
    prescribed_face_mask,
):
    number = interior_inverse.shape[0]
    squared_value = NFACE * NFACE
    solved = jnp.einsum(
        "eij,ejk->eik", interior_inverse, interior_to_face, preferred_element_type=jnp.float32
    ).astype(jnp.bfloat16)
    coupled = jnp.einsum(
        "eij,ejk->eik", face_to_interior, solved, preferred_element_type=jnp.float32
    )
    eye_six = jnp.eye(6, dtype=jnp.float32)
    own = face_diag.astype(jnp.float32).reshape(number, 6, NFACE, NFACE)
    blocks = (
        -coupled.reshape(number, 6, NFACE, 6, NFACE)
        + own[:, :, :, None, :] * eye_six[None, :, None, :, None]
    )
    targets = orientation_map(face_orient)
    slots = jnp.arange(NFACE, dtype=jnp.int32)
    moves = (targets[:, :, None, :] == slots[None, None, :, None]).astype(jnp.float32)
    turned = jnp.einsum(
        "earn,eanbm,ebsm->eabrs", moves, blocks, moves, precision=lax.Precision.HIGHEST
    )
    contrib = turned.astype(jnp.bfloat16).reshape(number, 6, 6, squared_value)
    cell_order = jnp.argsort(element_cell)
    element_lattice = jnp.take(contrib, cell_order, axis=0).reshape(
        EX, EY, ELEMENTS_Z_PART, 6, 6, squared_value
    )
    row_list = []
    for direction in range(3):
        right_all = upper_neighbours(element_lattice, direction)
        row_list.append(
            assemble(
                element_lattice[:, :, :, 2 * direction + 1],
                right_all,
                direction,
                prescribed_face_mask,
            )
        )
    rows = jnp.stack(row_list, axis=3).reshape(F_DEV, 11, squared_value)
    send_order = jnp.argsort(face_owner.reshape(F_DEV))
    outgoing = jnp.take(rows, send_order, axis=0)
    own_index = lax.axis_index("gz")
    share = F_DEV // lax.axis_size("gz")
    places = jnp.arange(F_DEV, dtype=jnp.int32)
    piece = lax.all_gather(outgoing, "gz", axis=0, tiled=True)
    spots = jnp.arange(piece.shape[0], dtype=jnp.int32)
    source = spots // F_DEV
    within = spots % F_DEV
    target = source * share + within % share
    wanted = within // share == own_index
    picker = ((places[:, None] == target[None, :]) & wanted[None, :]).astype(jnp.bfloat16)
    received = jnp.einsum("ji,ikl->jkl", picker, piece, preferred_element_type=jnp.float32).astype(
        jnp.bfloat16
    )
    return received.reshape(1, 1, F_DEV, 11, squared_value)


def solution(mesh):
    return jax.shard_map(
        shards,
        mesh=mesh,
        in_specs=(
            P(("gx", "gy", "gz"), None, None),
            P(("gx", "gy", "gz"), None, None),
            P(("gx", "gy", "gz"), None, None),
            P(("gx", "gy", "gz"), None, None),
            P(("gx", "gy", "gz")),
            P(("gx", "gy", "gz"), None),
            P("gx", "gy", "gz", None),
            P("gx", "gy", "gz", None),
        ),
        out_specs=P("gx", "gy", "gz", None, None),
        check_vma=False,
    )
```

profile of v0, /device:TPU:1, one launch (start us, length us, event | category | flops | bytes accessed | tf_op | source)
XLA Modules:
  0.0 330.6 jit_solution(6754147127760350506)
XLA Ops:
  6.6 1.8 sort.35
  8.3 0.7 fusion.35
  9.1 9.3 %negate_bitcast_fusion = f32[8,384,384]{1,2,0:T(8,128)} fusion(bf16[8,384,512]{2,1,0:T(8,128)(2,1)S(1)} %copy-done, bf16[8,512,512]{2,1,0:T(8,128)(2,1)} %param.8, bf16[8,512,384]{2,1,0:T(8,128)(2,1)} %param.9), kind=kOutput, calls=%fused_computation.8 | convolution fusion | flops 2821324800 | bytes 15204352 | tf_op jit(solution)/shard_map/eij,ejk->eik/dot_general | solution.py:88
  18.3 6.2 %copy.35 = f32[8,384,384]{2,1,0:T(8,128)} copy(f32[8,384,384]{1,2,0:T(8,128)} %negate_bitcast_fusion) | data formatting | bytes 9437184 | tf_op jit(solution)/shard_map/neg | solution.py:94
  24.5 9.3 %neg.11 = f32[8,6,64,6,64]{4,3,2,1,0:T(8,128)} reshape(f32[8,384,384]{2,1,0:T(8,128)} %copy.35) | data formatting | bytes 9437184 | tf_op jit(solution)/shard_map/neg | solution.py:94
  33.8 0.6 reshape.380
  34.4 12.0 %multiply_add_fusion = f32[8,6,64,6,64]{4,3,2,1,0:T(8,128)} fusion(f32[8,6,64,6,64]{4,3,2,1,0:T(8,128)} %neg.11, f32[6,6]{1,0:T(8,128)S(1)} %fusion.41, f32[8,6,64,64]{3,2,0,1:T(8,128)S(1)} %reshape.380), kind=kLoop, calls=%fused_computation.2 | loop fusion | flops 2359296 | bytes 10223760 | tf_op jit(solution)/shard_map/add | solution.py:94
  46.4 0.1 fusion.29
  46.5 14.4 %fusion = f32[8,6,6,64,64]{3,4,1,2,0:T(8,128)} fusion(f32[8,6,64,6,64]{4,3,2,1,0:T(8,128)} %multiply_add_fusion, s32[8,6,64]{2,1,0:T(8,128)S(1)} %fusion.29), kind=kOutput, calls=%fused_computation.3 | convolution fusion | flops 906166272 | bytes 9449472 | tf_op jit(solution)/shard_map/earn,eanbm,ebsm->eabrs/dot_general | solution.py:100
  60.9 9.2 %convert_bitcast_fusion = bf16[8,6,6,64,64]{4,3,1,2,0:T(8,128)(2,1)} fusion(f32[8,6,6,64,64]{3,4,1,2,0:T(8,128)} %fusion, s32[8,6,64]{2,1,0:T(8,128)S(1)} %fusion.29), kind=kOutput, calls=%fused_computation.7 | convolution fusion | flops 907345920 | bytes 7090176 | tf_op jit(solution)/shard_map/earn,eanbm,ebsm->eabrs/dot_general | solution.py:100
  70.1 8.0 %reshape.401 = bf16[8,6,6,4096]{3,1,2,0:T(8,128)(2,1)} reshape(bf16[8,6,6,64,64]{4,3,1,2,0:T(8,128)(2,1)} %convert_bitcast_fusion) | data formatting | bytes 4718592 | tf_op jit(solution)/shard_map/reshape | solution.py:103
  78.1 3.4 %copy.40 = bf16[8,6,6,4096]{3,2,1,0:T(8,128)(2,1)S(1)} copy(bf16[8,6,6,4096]{3,1,2,0:T(8,128)(2,1)} %reshape.401) | data formatting | bytes 4718592 | tf_op jit(solution)/shard_map/reshape | solution.py:103
  81.6 0.1 reshape.376
  81.7 1.6 sort.34
  83.3 0.5 copy-done.12
  83.8 0.1 broadcast_in_dim.112
  83.9 2.4 gather_fusion
  86.3 4.8 %broadcast_select_fusion = bf16[2,2,2,6,6,4096]{5,2,4,1,0,3:T(2,128)(2,1)S(1)} fusion(pred[2,2,2]{2,1,0:T(4,128)(4,1)S(1)} %broadcast_in_dim.112, bf16[2,2,2,6,6,4096]{5,4,3,2,1,0:T(8,128)(2,1)} %bitcast.93), kind=kLoop, calls=%fused_computation.9 | loop fusion | flops 1179648 | bytes 4718600 | tf_op jit(solution)/shard_map/jit(_take)/select_n | solution.py:105
  91.1 3.0 slice_bitcast_fusion.4
  94.1 1.1 fusion.49
  95.2 3.2 collective-permute-start.1
  98.4 1.6 fusion.50
  100.0 2.3 collective-permute-start.2
  102.3 1.1 slice_bitcast_fusion.9
  103.5 2.7 collective-permute-start
  106.2 0.9 slice_bitcast_fusion.6
  107.1 0.7 slice_bitcast_fusion.11
  107.8 1.0 slice_bitcast_fusion.5
  108.9 0.3 compare_reduce_fusion.2
  109.2 0.1 convert_element_type.76
  109.3 1.2 compare_and_fusion.1
  110.5 1.0 fusion.25
  111.5 1.1 fusion.20
  112.6 1.0 fusion.22
  113.6 1.0 fusion.26
  114.6 0.6 fusion.17
  115.2 0.1 fusion.27
  115.4 0.9 fusion.23
  116.3 0.5 fusion.15
  116.8 0.1 fusion.21
  116.9 0.2 fusion.19
  117.2 3.1 broadcast_select_fusion.3
  120.3 3.7 %pad_maximum_fusion = bf16[2,2,2,3,11,4096]{5,2,4,1,0,3:T(2,128)(2,1)S(1)} fusion(bf16[2,2,2,1,11,4096]{5,2,4,1,0,3:T(2,128)(2,1)S(1)} %get-tuple-element.25, bf16[2,2,2,1,11,4096]{5,2,4,1,0,3:T(2,128)(2,1)S(1)} %get-tuple-element.24, bf16[2,2,2,1,11,4096]{5,2,4,1,0,3:T(2,128)(2,1)S(1)} %get-tuple-element.23), kind=kLoop, calls=%fused_computation.12 | loop fusion | flops 2162688 | bytes 4325376 | tf_op jit(solution)/shard_map/stack | solution.py:119
  124.0 1.7 copy.57
  125.7 2.5 gather_fusion.1
  128.2 5.7 %copy_select_fusion = bf16[24,11,4096]{2,0,1:T(8,128)(2,1)} fusion(bf16[24,11,4096]{2,1,0:T(8,128)(2,1)} %gather_fusion.1, pred[24]{0:T(512)(128)(4,1)S(1)} %copy-done.11), kind=kLoop, calls=%fused_computation.13 | loop fusion | flops 1081344 | bytes 4325400 | tf_op jit(solution)/shard_map/jit(_take)/select_n | solution.py:121
  134.0 179.5 %all-gather.2.cloned.1.call-done = bf16[192,11,4096]{2,0,1:T(8,128)(2,1)} async-done(((bf16[24,11,4096]{2,0,1:T(8,128)(2,1)}), bf16[192,11,4096]{2,0,1:T(8,128)(2,1)}) %all-gather.2.cloned.1.call-update) | async-done | bytes 17301520 | tf_op jit(solution)/shard_map/all_gather | solution.py:125
  313.5 9.8 %fusion.2 = bf16[1,1,24,11,4096]{4,2,3,1,0:T(8,128)(2,1)} fusion(bf16[192,11,4096]{2,0,1:T(8,128)(2,1)} %all-gather.2.cloned.1.call-done, s32[192]{0:T(256)S(1)} %fusion.47, pred[192]{0:T(512)(128)(4,1)S(1)} %fusion.48), kind=kOutput, calls=%fused_computation.6 | convolution fusion | flops 416326656 | bytes 19465152 | tf_op jit(solution)/shard_map/ji,ikl->jkl/dot_general | solution.py:132
  (42 shorter events, 0.2 us)
Async XLA Ops:
  6.5 2.5 copy-start
  6.5 307.0 %all-gather.2.cloned.1.call-start = ((), (), s32[]{:S(2)}) async-start(), calls=%async_computation | async-start | bytes 19464192 | tf_op jit(solution)/shard_map/all_gather | solution.py:125
  24.5 9.3 %copy-start.7 = (bf16[8,6,4096]{2,0,1:T(8,128)(2,1)S(1)}, bf16[8,6,4096]{2,0,1:T(8,128)(2,1)}, u32[]{:S(2)}) copy-start(bf16[8,6,4096]{2,0,1:T(8,128)(2,1)} %param.11) | copy-start | bytes 1179652
  78.1 3.4 %copy-start.10 = (s32[2,2,2,3]{3,2,1,0:T(2,128)S(1)}, s32[2,2,2,3]{3,2,1,0:T(2,128)}, u32[]{:S(2)}) copy-start(s32[2,2,2,3]{3,2,1,0:T(2,128)} %param.14) | copy-start | bytes 292
  83.3 0.5 copy-start.12
  94.1 13.7 %copy-start.3 = (bf16[2,2,2,6,4096]{4,2,3,1,0:T(2,128)(2,1)}, bf16[2,2,2,6,4096]{4,2,3,1,0:T(2,128)(2,1)S(1)}, u32[]{:S(2)}) copy-start(bf16[2,2,2,6,4096]{4,2,3,1,0:T(2,128)(2,1)S(1)} %get-tuple-element.14) | copy-start | bytes 1179652
  94.1 14.8 %copy-start.4 = (bf16[2,2,2,6,4096]{4,2,3,1,0:T(2,128)(2,1)}, bf16[2,2,2,6,4096]{4,2,3,1,0:T(2,128)(2,1)S(1)}, u32[]{:S(2)}) copy-start(bf16[2,2,2,6,4096]{4,2,3,1,0:T(2,128)(2,1)S(1)} %get-tuple-element.12) | copy-start | bytes 1179652
  94.1 14.8 %copy-start.9 = (s32[2,2,2,3]{3,2,1,0:T(2,128)S(1)}, s32[2,2,2,3]{3,2,1,0:T(2,128)}, u32[]{:S(2)}) copy-start(s32[2,2,2,3]{3,2,1,0:T(2,128)} %param.15) | copy-start | bytes 292
  95.2 15.3 %collective-permute-start.1 = (bf16[2,1,2,6,4096]{4,2,3,1,0:T(2,128)(2,1)}, bf16[2,1,2,6,4096]{4,2,3,1,0:T(2,128)(2,1)S(1)}, u32[]{:S(2)}, u32[]{:S(2)}) collective-permute-start(bf16[2,1,2,6,4096]{4,2,3,1,0:T(2,128)(2,1)} %get-tuple-element.20), channel_id=1, source_target_pairs={{0,56},{8,0},{16,8},{24,16},{32,24},{40,32},{48,40},{56,48},{1,57}... | collective-permute-start | bytes 589832 | tf_op jit(solution)/shard_map/ppermute | solution.py:17
  100.0 13.6 %collective-permute-start.2 = (bf16[2,2,1,6,4096]{4,2,3,1,0:T(2,128)(2,1)}, bf16[2,2,1,6,4096]{4,2,3,1,0:T(2,128)(2,1)S(1)}, u32[]{:S(2)}, u32[]{:S(2)}) collective-permute-start(bf16[2,2,1,6,4096]{4,2,3,1,0:T(2,128)(2,1)} %get-tuple-element.22), channel_id=1, source_target_pairs={{0,7},{1,0},{2,1},{3,2},{4,3},{5,4},{6,5},{7,6},{8,15},{9,8},{10,9... | collective-permute-start | bytes 589832 | tf_op jit(solution)/shard_map/ppermute | solution.py:17
  103.5 11.9 %copy-start.2 = (bf16[1,2,2,6,4096]{4,2,3,1,0:T(2,128)(2,1)S(1)}, bf16[1,2,2,6,4096]{4,2,3,1,0:T(2,128)(2,1)}, u32[]{:S(2)}) copy-start(bf16[1,2,2,6,4096]{4,2,3,1,0:T(2,128)(2,1)} %get-tuple-element.17) | copy-start | bytes 589828
  103.5 11.9 %collective-permute-start = (bf16[1,2,2,6,4096]{4,2,3,1,0:T(2,128)(2,1)}, bf16[1,2,2,6,4096]{4,2,3,1,0:T(2,128)(2,1)S(1)}, u32[]{:S(2)}, u32[]{:S(2)}) collective-permute-start(bf16[1,2,2,6,4096]{4,2,3,1,0:T(2,128)(2,1)} %get-tuple-element.18), channel_id=1, source_target_pairs={{0,192},{64,0},{128,64},{192,128},{1,193},{65,1},{129,65},{193,129... | collective-permute-start | bytes 589832 | tf_op jit(solution)/shard_map/ppermute | solution.py:17
  110.5 6.7 %copy-start.5 = (bf16[2,2,2,1,5,4096]{5,2,4,1,0,3:T(2,128)(2,1)S(1)}, bf16[2,2,2,1,5,4096]{5,2,4,1,0,3:T(2,128)(2,1)}, u32[]{:S(2)}) copy-start(bf16[2,2,2,1,5,4096]{5,2,4,1,0,3:T(2,128)(2,1)} %slice_bitcast_fusion.5) | copy-start | bytes 983044
  110.5 6.7 %copy-start.6 = (bf16[2,2,2,1,4,4096]{5,2,4,1,0,3:T(2,128)(2,1)S(1)}, bf16[2,2,2,1,4,4096]{5,2,4,1,0,3:T(2,128)(2,1)}, u32[]{:S(2)}) copy-start(bf16[2,2,2,1,4,4096]{5,2,4,1,0,3:T(2,128)(2,1)} %slice_bitcast_fusion.6) | copy-start | bytes 786436
  110.5 6.7 %copy-start.8 = (bf16[2,2,2,1,1,4096]{5,2,4,1,0,3:T(2,128)(2,1)S(1)}, bf16[2,2,2,1,1,4096]{5,2,4,1,0,3:T(2,128)(2,1)}, u32[]{:S(2)}) copy-start(bf16[2,2,2,1,1,4096]{5,2,4,1,0,3:T(2,128)(2,1)} %slice_bitcast_fusion.11) | copy-start | bytes 196612
  125.7 2.5 copy-start.11
  313.5 9.8 %copy-start.1 = (bf16[8,384,512]{2,1,0:T(8,128)(2,1)S(1)}, bf16[8,384,512]{2,1,0:T(8,128)(2,1)}, u32[]{:S(2)}) copy-start(bf16[8,384,512]{2,1,0:T(8,128)(2,1)} %param.10) | copy-start | bytes 9437188
Sparse Core Ops, SparseCore 0:
  134.1 179.3 all-gather.1
where the time goes:
time: 335 us; the launch traced here: 331 us
  waiting for transfers between devices  180 us (54%)
  local copies, waits for them, and re-layouts  46.4 us (14%)
  matrix products  42.6 us (13%)
  other arithmetic  39.6 us (12%)
  between operations  14.1 us (4%)
  starting transfers between devices  8.31 us (2%)
    all_gather x1, waiting for transfers between devices, shards(): piece = lax.all_gather(outgoing, 'gz', axis=0, tiled=True)  180 us
    dot_general x2, matrix products, shards(): jnp.einsum('earn,eanbm,ebsm->eabrs', moves, blocks, moves, precision=lax....  23.6 us
    neg x2, local copies, waits for them, and re-layouts, shards(): -coupled.reshape(number, 6, NFACE, 6, NFACE)  15.5 us
    add x1, other arithmetic, shards(): -coupled.reshape(number, 6, NFACE, 6, NFACE)  12 us
    reshape x2, local copies, waits for them, and re-layouts, shards(): contrib = turned.astype(jnp.bfloat16).reshape(number, 6, 6, squared_value)  11.4 us
    dot_general x1, matrix products, shards(): jnp.einsum('ji,ikl->jkl', picker, piece, preferred_element_type=jnp.float32)  9.76 us
    dot_general x1, matrix products, shards(): jnp.einsum('eij,ejk->eik', face_to_interior, solved, preferred_element_ty...  9.26 us
    ppermute x3, starting transfers between devices, shifted(): return lax.ppermute(value, axis, pairs)  8.3 us
  transfers between devices with their start and end apart: 4, of which 1 were waited for; matrix products, arithmetic and copies ran while one was open for 4% of the time, Pallas kernels for 0%

commit v1 on v0

v1 whole, which is shorter than its diff:
```python
import jax
import jax.numpy as jnp
from jax import lax
from jax.experimental import pallas as pl
from jax.experimental.pallas import tpu as pltpu
from jax.sharding import PartitionSpec as P

Q = 8
NFACE = 64
NINT = 512
FACES = 6
WIDTH = FACES * NFACE
E_DEV = 8
F_DEV = 24
PER = 3
HALF = 32
LANES = 128
MESH = pl.DeviceIdType.MESH
F32 = jnp.float32
BF16 = jnp.bfloat16


def iota(shape, axis):
    return lax.broadcasted_iota(jnp.int32, shape, axis)


def mapped_nodes(nodes, codes):
    first, second = nodes // Q, nodes % Q
    swapped = codes // 4 % 2 == 1
    new_first = jnp.where(swapped, second, first)
    new_second = jnp.where(swapped, first, second)
    new_first = jnp.where(codes % 2 == 1, Q - 1 - new_first, new_first)
    new_second = jnp.where(codes // 2 % 2 == 1, Q - 1 - new_second, new_second)
    return Q * new_first + new_second


def condense_kernel(
    cell_ref,
    orient_ref,
    owner_ref,
    inverse_ref,
    to_face_ref,
    to_interior_ref,
    diag_ref,
    contrib_ref,
    slot_ref,
    diag_rows,
):
    e = pl.program_id(0)

    @pl.when(e == 0)
    def _():
        for f in range(F_DEV):
            slot_ref[owner_ref[f // 12, f // 6 % 2, f // 3 % 2, f % 3]] = f

    diag = diag_ref[0].astype(F32)
    for r in range(HALF):
        diag_rows[pl.ds(r, FACES, stride=HALF), :] = diag[:, r * LANES : (r + 1) * LANES]

    solved = jnp.dot(inverse_ref[0], to_face_ref[0], preferred_element_type=F32).astype(BF16)

    lane = iota((1, LANES), 1)
    row = iota((LANES, LANES), 0)
    col = iota((LANES, LANES), 1)
    row_node = 2 * (row % HALF) + row // HALF % 2 + NFACE * (row // NFACE)
    wide = iota((2 * LANES, LANES), 0)
    wide_node = wide % NFACE + NFACE * (wide // LANES)
    half_nodes = 2 * (lane % HALF) + lane // NFACE
    same_face = row // NFACE == col // NFACE
    low = col < NFACE

    turned_rows = []
    col_moves = []
    own = []
    for p in range(3):
        code_a, code_b = orient_ref[e, 2 * p], orient_ref[e, 2 * p + 1]
        second = lane // NFACE
        codes = jnp.where(second == 1, code_b, code_a)
        target = mapped_nodes(lane % NFACE, codes) + NFACE * second
        row_move = (target == row_node).astype(BF16)
        col_moves.append((target == wide_node).astype(BF16))
        face_rows = to_interior_ref[0, p * LANES : (p + 1) * LANES, :]
        turned_rows.append(jnp.dot(row_move, face_rows, preferred_element_type=F32).astype(BF16))
        second = lane // HALF % 2
        codes = jnp.where(second == 1, code_b, code_a)
        target = mapped_nodes(half_nodes, codes) + NFACE * second
        move = (target == row_node).astype(BF16)
        pair = diag_rows[p * NFACE : (p + 1) * NFACE, :]
        low_pair = low[:NFACE]
        stacked = jnp.concatenate(
            [jnp.where(low_pair, pair, 0.0), jnp.where(low_pair, 0.0, pair)], axis=0
        ).astype(BF16)
        moved = jnp.dot(move, stacked, preferred_element_type=F32)
        moved = moved + pltpu.roll(moved, NFACE, 1)
        own.append(jnp.where(same_face, moved, 0.0))

    for a in range(3):
        coupled = jnp.dot(turned_rows[a], solved, preferred_element_type=F32)
        for p in range(3):
            block = -coupled[:, p * LANES : (p + 1) * LANES]
            if p == a:
                block = block + own[p]
            block = lax.dot_general(
                block.astype(BF16),
                col_moves[p],
                (((1,), (1,)), ((), ())),
                preferred_element_type=F32,
            )
            even_lanes = iota((HALF, 2 * LANES), 1) % LANES < NFACE
            for s in range(2):
                top = block[s * NFACE : s * NFACE + HALF]
                bottom = block[s * NFACE + HALF : (s + 1) * NFACE]
                merged = jnp.where(even_lanes, top, bottom).astype(BF16)
                contrib_ref[0, 2 * a + s, 2 * p] = merged[:, :LANES]
                contrib_ref[0, 2 * a + s, 2 * p + 1] = merged[:, LANES:]


def condense(inverse, to_face, to_interior, diag, cells, orient, owner):
    number = inverse.shape[0]
    grid_spec = pltpu.PrefetchScalarGridSpec(
        num_scalar_prefetch=3,
        grid=(number,),
        in_specs=[
            pl.BlockSpec((1, NINT, NINT), lambda e, cell, o, w: (e, 0, 0)),
            pl.BlockSpec((1, NINT, WIDTH), lambda e, cell, o, w: (e, 0, 0)),
            pl.BlockSpec((1, WIDTH, NINT), lambda e, cell, o, w: (e, 0, 0)),
            pl.BlockSpec((1, FACES, NFACE * NFACE), lambda e, cell, o, w: (e, 0, 0)),
        ],
        out_specs=[
            pl.BlockSpec(
                (1, FACES, FACES, HALF, LANES), lambda e, cell, o, w: (cell[e], 0, 0, 0, 0)
            ),
            pl.BlockSpec(memory_space=pltpu.SMEM),
        ],
        scratch_shapes=[pltpu.VMEM((FACES * HALF, LANES), F32)],
    )
    return pl.pallas_call(
        condense_kernel,
        grid_spec=grid_spec,
        out_shape=[
            jax.ShapeDtypeStruct((number, FACES, FACES, HALF, LANES), BF16),
            jax.ShapeDtypeStruct((F_DEV,), jnp.int32),
        ],
        compiler_params=pltpu.CompilerParams(
            dimension_semantics=("arbitrary",), vmem_limit_bytes=32 << 20
        ),
        name="condense",
    )(cells, orient, owner, inverse, to_face, to_interior, diag)


def exchange_kernel(
    counts,
    slot_ref,
    flag_ref,
    c_ref,
    out_ref,
    right,
    stage,
    landed,
    flat,
    halo_send,
    halo_recv,
    send,
    recv,
):
    n_gx, n_gy, n_gz = counts
    gx, gy, gz = lax.axis_index("gx"), lax.axis_index("gy"), lax.axis_index("gz")
    below = (
        {"gx": lax.rem(gx + n_gx - 1, n_gx)},
        {"gy": lax.rem(gy + n_gy - 1, n_gy)},
        {"gz": lax.rem(gz + n_gz - 1, n_gz)},
    )
    above = ({"gx": lax.rem(gx + 1, n_gx)}, {"gy": lax.rem(gy + 1, n_gy)})

    barrier = pltpu.get_barrier_semaphore()
    greeted = [below[0], below[1], above[0], above[1]]
    greeted += [{"gz": lax.rem(gz + k, n_gz)} for k in range(1, n_gz)]
    for device in greeted:
        pl.semaphore_signal(barrier, inc=1, device_id=device, device_id_type=MESH)
    pl.semaphore_wait(barrier, len(greeted))

    halo = []
    for d in range(3):
        source = (c_ref.at[0, :, :, 0], c_ref.at[:, 0, :, 2], c_ref.at[:, :, 0, 4])[d]
        place = (right.at[0, 1], right.at[1, :, 1], right.at[2, :, :, 1])[d]
        copy = pltpu.make_async_remote_copy(
            src_ref=source,
            dst_ref=place,
            send_sem=halo_send.at[d],
            recv_sem=halo_recv.at[d],
            device_id=below[d],
            device_id_type=MESH,
        )
        copy.start()
        halo.append(copy)

    def face_of(k, j):
        place = PER * lax.rem(gz + k, n_gz) + j
        f = slot_ref[place]
        cell, d = f // 3, f % 3
        cx, cy, cz = cell // 4, cell // 2 % 2, cell % 2
        keep = 1 - flag_ref[cx, cy, cz, d]
        return cx, cy, cz, d, keep

    def stage_left(k):
        for j in range(PER):
            cx, cy, cz, d, keep = face_of(k, j)
            scale = jnp.full((HALF, LANES), keep, jnp.int32).astype(F32).astype(BF16)
            for b in range(5):
                other = b + (b >= 2 * d + 1).astype(jnp.int32)
                stage[k, j, b] = c_ref[cx, cy, cz, 2 * d + 1, other] * scale

    diagonal = (
        iota((HALF, LANES), 1) % NFACE == 2 * iota((HALF, LANES), 0) + iota((HALF, LANES), 1) // NFACE
    ).astype(F32)

    def stage_right(k):
        for j in range(PER):
            cx, cy, cz, d, keep = face_of(k, j)
            wide = jnp.full((HALF, LANES), keep, jnp.int32).astype(F32)
            scale = wide.astype(BF16)
            total = c_ref[cx, cy, cz, 2 * d + 1, 2 * d + 1].astype(F32) + right[
                d, cx, cy, cz, 2 * d
            ].astype(F32)
            stage[k, j, 5] = (total * wide + diagonal * (1.0 - wide)).astype(BF16)
            for b in range(5):
                other = b + (b >= 2 * d).astype(jnp.int32)
                stage[k, j, 6 + b] = right[d, cx, cy, cz, other] * scale

    def push(k, part):
        first, size = ((0, 5), (5, 6))[part]
        return pltpu.make_async_remote_copy(
            src_ref=stage.at[k, :, pl.ds(first, size)],
            dst_ref=landed.at[k, :, pl.ds(first, size)],
            send_sem=send.at[k, part],
            recv_sem=recv.at[k, part],
            device_id={"gz": lax.rem(gz + k, n_gz)},
            device_id_type=MESH,
        )

    @pl.loop(1, n_gz)
    def _(k):
        stage_left(k)
        push(k, 0).start()

    stage_left(0)

    @pl.loop(0, 2)
    def _(u):
        @pl.loop(0, 2)
        def _(w):
            right[0, 0, u, w] = c_ref[1, u, w, 0]
            right[1, u, 0, w] = c_ref[u, 1, w, 2]
            right[2, u, w, 0] = c_ref[u, w, 1, 4]

    for copy in halo:
        copy.wait_recv()

    @pl.loop(1, n_gz)
    def _(k):
        stage_right(k)
        push(k, 1).start()

    stage_right(0)

    def unfold(source, k):
        start = PER * lax.rem(gz - k + n_gz, n_gz)
        for j in range(PER):
            for b in range(11):
                to = b + 1 if b < 5 else (0 if b == 5 else b)
                flat[to * HALF : (to + 1) * HALF, :] = source[k, j, b].astype(F32)
            for r in range(HALF):
                out_ref[start + j, :, r * LANES : (r + 1) * LANES] = flat[
                    pl.ds(r, 11, stride=HALF), :
                ].astype(BF16)

    unfold(stage, 0)

    @pl.loop(1, n_gz)
    def _(k):
        push(k, 0).wait_recv()
        push(k, 1).wait_recv()
        unfold(landed, k)

    @pl.loop(1, n_gz)
    def _(k):
        push(k, 0).wait_send()
        push(k, 1).wait_send()

    for copy in halo:
        copy.wait_send()


def exchange(slots, flags, contrib, counts):
    n_gz = counts[2]
    vmem = pl.BlockSpec(memory_space=pltpu.VMEM)
    smem = pl.BlockSpec(memory_space=pltpu.SMEM)

    def body(*refs):
        exchange_kernel(counts, *refs)

    return pl.pallas_call(
        body,
        out_shape=jax.ShapeDtypeStruct((F_DEV, 11, NFACE * NFACE), BF16),
        in_specs=[smem, smem, vmem],
        out_specs=vmem,
        scratch_shapes=[
            pltpu.VMEM((3, 2, 2, 2, FACES, HALF, LANES), BF16),
            pltpu.VMEM((n_gz, PER, 11, HALF, LANES), BF16),
            pltpu.VMEM((n_gz, PER, 11, HALF, LANES), BF16),
            pltpu.VMEM((16 * HALF, LANES), F32),
            pltpu.SemaphoreType.DMA((3,)),
            pltpu.SemaphoreType.DMA((3,)),
            pltpu.SemaphoreType.DMA((n_gz, 2)),
            pltpu.SemaphoreType.DMA((n_gz, 2)),
        ],
        compiler_params=pltpu.CompilerParams(
            collective_id=0, has_side_effects=True, vmem_limit_bytes=48 << 20
        ),
        name="exchange",
    )(slots, flags, contrib)


def shards(
    interior_inverse,
    interior_to_face,
    face_to_interior,
    face_diag,
    element_cell,
    face_orient,
    face_owner,
    prescribed_face_mask,
):
    contrib, slots = condense(
        interior_inverse,
        interior_to_face,
        face_to_interior,
        face_diag,
        element_cell,
        face_orient,
        face_owner,
    )
    counts = (lax.axis_size("gx"), lax.axis_size("gy"), lax.axis_size("gz"))
    contrib = contrib.reshape(2, 2, 2, FACES, FACES, HALF, LANES)
    rows = exchange(slots, prescribed_face_mask, contrib, counts)
    return rows.reshape(1, 1, F_DEV, 11, NFACE * NFACE)


def solution(mesh):
    return jax.shard_map(
        shards,
        mesh=mesh,
        in_specs=(
            P(("gx", "gy", "gz"), None, None),
            P(("gx", "gy", "gz"), None, None),
            P(("gx", "gy", "gz"), None, None),
            P(("gx", "gy", "gz"), None, None),
            P(("gx", "gy", "gz")),
            P(("gx", "gy", "gz"), None),
            P("gx", "gy", "gz", None),
            P("gx", "gy", "gz", None),
        ),
        out_specs=P("gx", "gy", "gz", None, None),
        check_vma=False,
    )
```

time: 335 us -> 62.7 us (0.19)
  the two profiles are of different devices: /device:TPU:1 before, /device:TPU:70 now
where the time goes in v1:
time: 62.7 us; the launch traced here: 62.1 us
  Pallas kernels  50.3 us (80%)
  local copies, waits for them, and re-layouts  11.8 us (19%)
    pallas_call x1, Pallas kernels, exchange(): pl.pallas_call(body, out_shape=jax.ShapeDtypeStruct((F_DEV, 11, NFACE * N...  39.6 us
    pallas_call x1, Pallas kernels, condense(): pl.pallas_call(condense_kernel, grid_spec=grid_spec, out_shape=[jax.Shape...  10.7 us
    unnamed x15, local copies, waits for them, and re-layouts  9.21 us
    reshape x1, local copies, waits for them, and re-layouts, shards(): return rows.reshape(1, 1, F_DEV, 11, NFACE * NFACE)  2.63 us

profile of v1, /device:TPU:70, one launch (start us, length us, event | category | flops | bytes accessed | tf_op | source)
XLA Modules:
  0.0 62.1 jit_solution(17653629718696569628)
XLA Ops:
  0.0 1.2 %copy.9.diag_ref = bf16[8,6,4096]{2,1,0:T(8,128)(2,1)S(1)} copy(bf16[8,6,4096]{2,0,1:T(8,128)(2,1)} %param.11) | data formatting | bytes 786432 | tf_op args[3]
  1.2 0.0 copy-start
  1.2 2.2 %copy-done = bf16[8,512,512]{2,1,0:T(8,128)(2,1)S(1)} copy-done((bf16[8,512,512]{2,1,0:T(8,128)(2,1)S(1)}, bf16[8,512,512]{2,1,0:T(8,128)(2,1)}, u32[]{:S(2)}) %copy-start) | copy-done | bytes 4194328
  3.4 0.0 copy-start.1
  3.4 1.9 %copy-done.1 = bf16[8,512,384]{2,1,0:T(8,128)(2,1)S(1)} copy-done((bf16[8,512,384]{2,1,0:T(8,128)(2,1)S(1)}, bf16[8,512,384]{2,1,0:T(8,128)(2,1)}, u32[]{:S(2)}) %copy-start.1) | copy-done | bytes 3145752
  5.3 0.0 copy-start.2
  5.3 1.9 %copy-done.2 = bf16[8,384,512]{2,1,0:T(8,128)(2,1)S(1)} copy-done((bf16[8,384,512]{2,1,0:T(8,128)(2,1)S(1)}, bf16[8,384,512]{2,1,0:T(8,128)(2,1)}, u32[]{:S(2)}) %copy-start.2) | copy-done | bytes 3145752
  7.2 0.0 copy-start.3
  7.2 0.7 %copy-done.3 = s32[8,6]{1,0:T(8,128)S(1)} copy-done((s32[8,6]{1,0:T(8,128)S(1)}, s32[8,6]{1,0:T(8,128)}, u32[]{:S(2)}) %copy-start.3) | copy-done | bytes 216
  7.9 0.0 copy-start.4
  7.9 0.7 %copy-done.4 = s32[2,2,2,3]{3,2,1,0:T(2,128)S(1)} copy-done((s32[2,2,2,3]{3,2,1,0:T(2,128)S(1)}, s32[2,2,2,3]{3,2,1,0:T(2,128)}, u32[]{:S(2)}) %copy-start.4) | copy-done | bytes 120
  8.6 0.0 copy-start.6
  8.6 0.7 %copy-done.6 = s32[8]{0:T(128)S(1)} copy-done((s32[8]{0:T(128)S(1)}, s32[8]{0:T(128)}, u32[]{:S(2)}) %copy-start.6) | copy-done | bytes 56
  9.2 0.0 copy-start.5
  9.2 10.7 %condense.1 = (bf16[8,6,6,32,128]{4,3,2,1,0:T(8,128)(2,1)S(1)}, s32[24]{0:T(128)S(1)}) custom-call(s32[8]{0:T(128)S(1)} %copy-done.6, s32[8,6]{1,0:T(8,128)S(1)} %copy-done.3, s32[2,2,2,3]{3,2,1,0:T(2,128)S(1)} %copy-done.4, bf16[8,512,512]{2,1,0:T(8,128)(2,1)S(1)} %copy-done, bf16[8,512,384]{2,1,0:T(8,128)(2,1)S(1)} %copy-done.1, ...), custom_call_target="tpu_custom_call" | custom-call | tf_op jit(solution)/shard_map/condense/pallas_call | solution.py:137
  19.9 0.0 copy-done.5
  19.9 39.6 %exchange.1 = bf16[24,11,4096]{2,1,0:T(8,128)(2,1)S(1)} custom-call(s32[24]{0:T(128)S(1)} %get-tuple-element.7.refs_0_, s32[2,2,2,3]{3,2,1,0:T(2,128)S(1)} %copy-done.5, bf16[2,2,2,6,6,32,128]{6,5,4,3,2,1,0:T(8,128)(2,1)S(1)} %bitcast.3), custom_call_target="tpu_custom_call" | custom-call | tf_op jit(solution)/shard_map/exchange/pallas_call | solution.py:302
  59.5 2.6 %copy.10 = bf16[1,1,24,11,4096]{4,2,3,1,0:T(8,128)(2,1)} copy(bf16[1,1,24,11,4096]{4,3,2,1,0:T(8,128)(2,1)S(1)} %bitcast.2) | data formatting | bytes 4325376 | tf_op jit(solution)/shard_map/reshape | solution.py:346
Async XLA Ops:
  1.2 2.2 %copy-start = (bf16[8,512,512]{2,1,0:T(8,128)(2,1)S(1)}, bf16[8,512,512]{2,1,0:T(8,128)(2,1)}, u32[]{:S(2)}) copy-start(bf16[8,512,512]{2,1,0:T(8,128)(2,1)} %inverse_ref.1) | copy-start | bytes 12582916
  3.4 1.9 %copy-start.1 = (bf16[8,512,384]{2,1,0:T(8,128)(2,1)S(1)}, bf16[8,512,384]{2,1,0:T(8,128)(2,1)}, u32[]{:S(2)}) copy-start(bf16[8,512,384]{2,1,0:T(8,128)(2,1)} %to_face_ref.1) | copy-start | bytes 9437188
  5.3 1.9 %copy-start.2 = (bf16[8,384,512]{2,1,0:T(8,128)(2,1)S(1)}, bf16[8,384,512]{2,1,0:T(8,128)(2,1)}, u32[]{:S(2)}) copy-start(bf16[8,384,512]{2,1,0:T(8,128)(2,1)} %to_interior_ref.1) | copy-start | bytes 9437188
  7.2 0.7 %copy-start.3 = (s32[8,6]{1,0:T(8,128)S(1)}, s32[8,6]{1,0:T(8,128)}, u32[]{:S(2)}) copy-start(s32[8,6]{1,0:T(8,128)} %orient_ref.1) | copy-start | bytes 580
  7.9 0.7 %copy-start.4 = (s32[2,2,2,3]{3,2,1,0:T(2,128)S(1)}, s32[2,2,2,3]{3,2,1,0:T(2,128)}, u32[]{:S(2)}) copy-start(s32[2,2,2,3]{3,2,1,0:T(2,128)} %owner_ref.1) | copy-start | bytes 292
  8.6 0.7 %copy-start.6 = (s32[8]{0:T(128)S(1)}, s32[8]{0:T(128)}, u32[]{:S(2)}) copy-start(s32[8]{0:T(128)} %cell_ref.1) | copy-start | bytes 100
  9.2 10.7 %copy-start.5 = (s32[2,2,2,3]{3,2,1,0:T(2,128)S(1)}, s32[2,2,2,3]{3,2,1,0:T(2,128)}, u32[]{:S(2)}) copy-start(s32[2,2,2,3]{3,2,1,0:T(2,128)} %refs_1_.1) | copy-start | bytes 292

commit v2 on v0

v2 whole, which is shorter than its diff:
```python
import jax
import jax.numpy as jnp
from jax import lax
from jax.experimental import pallas as pl
from jax.experimental.pallas import tpu as pltpu
from jax.sharding import PartitionSpec as P

Q = 8
NFACE = 64
NINT = 512
FACES = 6
WIDTH = FACES * NFACE
E_DEV = 8
F_DEV = 24
PER = 3
HALF = 32
LANES = 128
MESH = pl.DeviceIdType.MESH
F32 = jnp.float32
BF16 = jnp.bfloat16


def iota(shape, axis):
    return lax.broadcasted_iota(jnp.int32, shape, axis)


def mapped_nodes(nodes, codes):
    first, second = nodes // Q, nodes % Q
    swapped = codes // 4 % 2 == 1
    new_first = jnp.where(swapped, second, first)
    new_second = jnp.where(swapped, first, second)
    new_first = jnp.where(codes % 2 == 1, Q - 1 - new_first, new_first)
    new_second = jnp.where(codes // 2 % 2 == 1, Q - 1 - new_second, new_second)
    return Q * new_first + new_second


def turn_rows(e, orient_ref, to_interior, diag_rows, own):
    lane = iota((1, LANES), 1)
    row = iota((LANES, LANES), 0)
    col = iota((LANES, LANES), 1)
    row_node = 2 * (row % HALF) + row // HALF % 2 + NFACE * (row // NFACE)
    half_nodes = 2 * (lane % HALF) + lane // NFACE
    same_face = row // NFACE == col // NFACE
    low = col[:NFACE] < NFACE
    for p in range(3):
        code_a, code_b = orient_ref[e, 2 * p], orient_ref[e, 2 * p + 1]
        second = lane // NFACE
        codes = jnp.where(second == 1, code_b, code_a)
        target = mapped_nodes(lane % NFACE, codes) + NFACE * second
        move = (target == row_node).astype(BF16)
        at = slice(p * LANES, (p + 1) * LANES)
        turned = jnp.dot(move, to_interior[e, at, :], preferred_element_type=F32)
        to_interior[e, at, :] = turned.astype(BF16)
        second = lane // HALF % 2
        codes = jnp.where(second == 1, code_b, code_a)
        target = mapped_nodes(half_nodes, codes) + NFACE * second
        move = (target == row_node).astype(BF16)
        at = pl.multiple_of(e * FACES * HALF + p * NFACE, NFACE)
        pair = diag_rows[pl.ds(at, NFACE), :]
        stacked = jnp.concatenate(
            [jnp.where(low, pair, 0.0), jnp.where(low, 0.0, pair)], axis=0
        ).astype(BF16)
        moved = jnp.dot(move, stacked, preferred_element_type=F32)
        moved = moved + pltpu.roll(moved, NFACE, 1)
        own[e, p] = jnp.where(same_face, moved, 0.0)


def pair_of_columns(e, p, orient_ref, to_interior, solved, own, contrib):
    lane = iota((1, LANES), 1)
    second = lane // NFACE
    codes = jnp.where(second == 1, orient_ref[e, 2 * p + 1], orient_ref[e, 2 * p])
    target = mapped_nodes(lane % NFACE, codes) + NFACE * second
    wide = iota((2 * LANES, LANES), 0)
    move = (target == wide % NFACE + NFACE * (wide // LANES)).astype(BF16)
    columns = solved[e, :, p * LANES : (p + 1) * LANES]
    blocks = -jnp.dot(to_interior[e], columns, preferred_element_type=F32)
    parts = [blocks[a * LANES : (a + 1) * LANES] for a in range(3)]
    parts[p] = parts[p] + own[e, p]
    blocks = lax.dot_general(
        jnp.concatenate(parts, axis=0).astype(BF16),
        move,
        (((1,), (1,)), ((), ())),
        preferred_element_type=F32,
    )
    even_lanes = iota((HALF, LANES), 1) < NFACE
    for a in range(FACES):
        top = blocks[a * NFACE : a * NFACE + HALF]
        bottom = blocks[a * NFACE + HALF : (a + 1) * NFACE]
        for q in range(2):
            at = slice(q * LANES, (q + 1) * LANES)
            contrib[e, a, 2 * p + q] = jnp.where(even_lanes, top[:, at], bottom[:, at]).astype(BF16)


RUNS = ((0, 1), (1, 2), (3, 2), (5, 6))


def condense_kernel(
    counts,
    inverse_hbm,
    to_face_hbm,
    to_interior_hbm,
    diag_hbm,
    cell_hbm,
    orient_hbm,
    owner_hbm,
    flag_hbm,
    out_ref,
    inverse,
    to_face,
    to_interior,
    diag,
    cell_ref,
    orient_ref,
    owner_ref,
    flag_ref,
    element_ref,
    slot_ref,
    solved,
    diag_rows,
    own,
    contrib,
    rim,
    right,
    stage,
    landed,
    flat,
    arrive,
    small_arrive,
    halo_send,
    halo_recv,
    send,
    recv,
):
    n_gx, n_gy, n_gz = counts
    gx, gy, gz = lax.axis_index("gx"), lax.axis_index("gy"), lax.axis_index("gz")
    below = (
        {"gx": lax.rem(gx + n_gx - 1, n_gx)},
        {"gy": lax.rem(gy + n_gy - 1, n_gy)},
        {"gz": lax.rem(gz + n_gz - 1, n_gz)},
    )
    above = ({"gx": lax.rem(gx + 1, n_gx)}, {"gy": lax.rem(gy + 1, n_gy)})

    small = [
        pltpu.make_async_copy(source, place, small_arrive.at[i])
        for i, (source, place) in enumerate(
            (
                (owner_hbm, owner_ref),
                (cell_hbm, cell_ref),
                (orient_hbm, orient_ref),
                (flag_hbm, flag_ref),
                (diag_hbm, diag),
            )
        )
    ]
    for copy in small:
        copy.start()

    def input_of(e, i):
        source, place = ((inverse_hbm, inverse), (to_face_hbm, to_face), (to_interior_hbm, to_interior))[i]
        return pltpu.make_async_copy(source.at[e], place.at[e], arrive.at[e, i])

    for e in range(E_DEV):
        for i in range(3):
            input_of(e, i).start()

    barrier = pltpu.get_barrier_semaphore()
    greeted = [below[0], below[1], above[0], above[1]]
    greeted += [{"gz": lax.rem(gz + k, n_gz)} for k in range(1, n_gz)]
    for device in greeted:
        pl.semaphore_signal(barrier, inc=1, device_id=device, device_id_type=MESH)

    for copy in small:
        copy.wait()

    @pl.loop(0, E_DEV)
    def _(c):
        found = 0
        for e in range(E_DEV):
            found = jnp.where(cell_ref[e] == c, e, found)
        element_ref[c] = found

    @pl.loop(0, F_DEV)
    def _(v):
        found = 0
        for f in range(F_DEV):
            at = (f // 12, f // 6 % 2, f // 3 % 2, f % 3)
            found = jnp.where(owner_ref[at] == v, f, found)
        slot_ref[v] = found

    for a in range(FACES):
        faces = diag[a].astype(F32)
        for r in range(HALF):
            diag_rows[pl.ds(a * HALF + r, E_DEV, stride=FACES * HALF), :] = faces[
                :, r * LANES : (r + 1) * LANES
            ]

    @pl.loop(0, E_DEV // 2)
    def _(i):
        for e in (2 * i, 2 * i + 1):
            for n in range(3):
                input_of(e, n).wait()
        for e in (2 * i, 2 * i + 1):
            product = jnp.dot(inverse[e], to_face[e], preferred_element_type=F32)
            solved[e] = product.astype(BF16)
            turn_rows(e, orient_ref, to_interior, diag_rows, own)

    def columns(p):
        @pl.loop(0, E_DEV // 2)
        def _(i):
            for e in (2 * i, 2 * i + 1):
                pair_of_columns(e, p, orient_ref, to_interior, solved, own, contrib)

    def face_of(k, j):
        f = slot_ref[PER * lax.rem(gz + k, n_gz) + j]
        cell, d = f // 3, f % 3
        cx, cy, cz = cell // 4, cell // 2 % 2, cell % 2
        keep = 1 - flag_ref[cx, cy, cz, d]
        return cell, cx, cy, cz, d, keep

    def stage_left(k, run):
        first, size = RUNS[run]
        for j in range(PER):
            cell, _, _, _, d, keep = face_of(k, j)
            e = element_ref[cell]
            scale = jnp.full((HALF, LANES), keep, jnp.int32).astype(F32).astype(BF16)
            for b in range(first, first + size):
                other = b + (b >= 2 * d + 1).astype(jnp.int32)
                stage[k, j, b] = contrib[e, 2 * d + 1, other] * scale

    diagonal = (
        iota((HALF, LANES), 1) % NFACE == 2 * iota((HALF, LANES), 0) + iota((HALF, LANES), 1) // NFACE
    ).astype(F32)

    def stage_right(k):
        for j in range(PER):
            cell, cx, cy, cz, d, keep = face_of(k, j)
            e = element_ref[cell]
            wide = jnp.full((HALF, LANES), keep, jnp.int32).astype(F32)
            scale = wide.astype(BF16)
            total = contrib[e, 2 * d + 1, 2 * d + 1].astype(F32) + right[
                d, cx, cy, cz, 2 * d
            ].astype(F32)
            stage[k, j, 5] = (total * wide + diagonal * (1.0 - wide)).astype(BF16)
            for b in range(5):
                other = b + (b >= 2 * d).astype(jnp.int32)
                stage[k, j, 6 + b] = right[d, cx, cy, cz, other] * scale

    def push(k, run):
        first, size = RUNS[run]
        return pltpu.make_async_remote_copy(
            src_ref=stage.at[k, :, pl.ds(first, size)],
            dst_ref=landed.at[k, :, pl.ds(first, size)],
            send_sem=send.at[k, run],
            recv_sem=recv.at[k, run],
            device_id={"gz": lax.rem(gz + k, n_gz)},
            device_id_type=MESH,
        )

    def send_left(run):
        @pl.loop(1, n_gz)
        def _(k):
            stage_left(k, run)
            push(k, run).start()

        stage_left(0, run)

    columns(0)
    pl.semaphore_wait(barrier, len(greeted))
    send_left(0)
    columns(1)
    send_left(1)
    columns(2)

    for d in range(3):
        step = (4, 2, 1)[d]
        free = ((2, 1), (4, 1), (4, 2))[d]

        @pl.loop(0, 2)
        def _(u):
            @pl.loop(0, 2)
            def _(w):
                cell = free[0] * u + free[1] * w
                rim[d, u, w] = contrib[element_ref[cell], 2 * d]
                at = ((0, u, w), (u, 0, w), (u, w, 0))[d]
                right[(d, *at)] = contrib[element_ref[cell + step], 2 * d]

    halo = []
    for d in range(3):
        place = (right.at[0, 1], right.at[1, :, 1], right.at[2, :, :, 1])[d]
        copy = pltpu.make_async_remote_copy(
            src_ref=rim.at[d],
            dst_ref=place,
            send_sem=halo_send.at[d],
            recv_sem=halo_recv.at[d],
            device_id=below[d],
            device_id_type=MESH,
        )
        copy.start()
        halo.append(copy)

    send_left(2)

    for copy in halo:
        copy.wait_recv()

    @pl.loop(1, n_gz)
    def _(k):
        stage_right(k)
        push(k, 3).start()

    stage_right(0)

    rows_at = 11 * HALF

    def spread(source, k, first, size):
        start = PER * lax.rem(gz - k + n_gz, n_gz)
        for j in range(PER):
            for b in range(first, first + size):
                to = b + 1 if b < 5 else (0 if b == 5 else b)
                at = pl.multiple_of((start + j) * rows_at + to * HALF, HALF)
                flat[pl.ds(at, HALF), :] = source[k, j, b].astype(F32)

    def unfold(b):
        for r in range(HALF):
            out_ref[b, :, r * LANES : (r + 1) * LANES] = flat[
                pl.ds(b * HALF + r, F_DEV, stride=rows_at), :
            ].astype(BF16)

    spread(stage, 0, 0, 11)

    @pl.loop(1, n_gz)
    def _(k):
        for run in range(3):
            push(k, run).wait_recv()
        spread(landed, k, 0, 5)

    @pl.loop(1, 6)
    def _(b):
        unfold(b)

    @pl.loop(1, n_gz)
    def _(k):
        push(k, 3).wait_recv()
        spread(landed, k, 5, 6)

    unfold(0)

    @pl.loop(6, 11)
    def _(b):
        unfold(b)

    @pl.loop(1, n_gz)
    def _(k):
        for run in range(4):
            push(k, run).wait_send()

    for copy in halo:
        copy.wait_send()


def shards(
    interior_inverse,
    interior_to_face,
    face_to_interior,
    face_diag,
    element_cell,
    face_orient,
    face_owner,
    prescribed_face_mask,
):
    counts = (lax.axis_size("gx"), lax.axis_size("gy"), lax.axis_size("gz"))
    n_gz = counts[2]
    block = (HALF, LANES)

    def body(*refs):
        condense_kernel(counts, *refs)

    rows = pl.pallas_call(
        body,
        out_shape=jax.ShapeDtypeStruct((11, F_DEV, NFACE * NFACE), BF16),
        in_specs=[pl.BlockSpec(memory_space=pl.ANY)] * 8,
        out_specs=pl.BlockSpec(memory_space=pltpu.VMEM),
        scratch_shapes=[
            pltpu.VMEM((E_DEV, NINT, NINT), BF16),
            pltpu.VMEM((E_DEV, NINT, WIDTH), BF16),
            pltpu.VMEM((E_DEV, WIDTH, NINT), BF16),
            pltpu.VMEM((FACES, E_DEV, NFACE * NFACE), BF16),
            pltpu.SMEM((E_DEV,), jnp.int32),
            pltpu.SMEM((E_DEV, FACES), jnp.int32),
            pltpu.SMEM((2, 2, 2, 3), jnp.int32),
            pltpu.SMEM((2, 2, 2, 3), jnp.int32),
            pltpu.SMEM((E_DEV,), jnp.int32),
            pltpu.SMEM((F_DEV,), jnp.int32),
            pltpu.VMEM((E_DEV, NINT, WIDTH), BF16),
            pltpu.VMEM((E_DEV * FACES * HALF, LANES), F32),
            pltpu.VMEM((E_DEV, 3, LANES, LANES), F32),
            pltpu.VMEM((E_DEV, FACES, FACES, *block), BF16),
            pltpu.VMEM((3, 2, 2, FACES, *block), BF16),
            pltpu.VMEM((3, 2, 2, 2, FACES, *block), BF16),
            pltpu.VMEM((n_gz, PER, 11, *block), BF16),
            pltpu.VMEM((n_gz, PER, 11, *block), BF16),
            pltpu.VMEM((F_DEV * 11 * HALF, LANES), F32),
            pltpu.SemaphoreType.DMA((E_DEV, 3)),
            pltpu.SemaphoreType.DMA((5,)),
            pltpu.SemaphoreType.DMA((3,)),
            pltpu.SemaphoreType.DMA((3,)),
            pltpu.SemaphoreType.DMA((n_gz, 4)),
            pltpu.SemaphoreType.DMA((n_gz, 4)),
        ],
        compiler_params=pltpu.CompilerParams(
            collective_id=0, has_side_effects=True, vmem_limit_bytes=40 << 20
        ),
        name="condense",
    )(
        *(
            pltpu.with_memory_space_constraint(value, pltpu.HBM)
            for value in (
                interior_inverse,
                interior_to_face,
                face_to_interior,
                face_diag.transpose(1, 0, 2),
                element_cell,
                face_orient,
                face_owner,
                prescribed_face_mask,
            )
        )
    )
    return rows.transpose(1, 0, 2).reshape(1, 1, F_DEV, 11, NFACE * NFACE)


def solution(mesh):
    return jax.shard_map(
        shards,
        mesh=mesh,
        in_specs=(
            P(("gx", "gy", "gz"), None, None),
            P(("gx", "gy", "gz"), None, None),
            P(("gx", "gy", "gz"), None, None),
            P(("gx", "gy", "gz"), None, None),
            P(("gx", "gy", "gz")),
            P(("gx", "gy", "gz"), None),
            P("gx", "gy", "gz", None),
            P("gx", "gy", "gz", None),
        ),
        out_specs=P("gx", "gy", "gz", None, None),
        check_vma=False,
    )
```

time: 335 us -> 53.1 us (0.16)
  the two profiles are of different devices: /device:TPU:1 before, /device:TPU:70 now
where the time goes in v2:
time: 53.1 us
  Pallas kernels  51.7 us (97%)
  local copies, waits for them, and re-layouts  1.34 us (3%)
    pallas_call x1, Pallas kernels, shards(): pl.pallas_call(body, out_shape=jax.ShapeDtypeStruct((11, F_DEV, NFACE * N...  51.7 us
    unnamed x1, local copies, waits for them, and re-layouts  1.34 us

profile of v2, /device:TPU:70, one launch (start us, length us, event | category | flops | bytes accessed | tf_op | source)
XLA Modules:
  0.0 53.1 jit_solution(7640049175732472124)
XLA Ops:
  0.0 51.7 %condense.1 = bf16[11,24,4096]{2,1,0:T(8,128)(2,1)S(1)} custom-call(bf16[8,512,512]{2,1,0:T(8,128)(2,1)} %refs_0_.1, bf16[8,512,384]{2,1,0:T(8,128)(2,1)} %refs_1_.1, bf16[8,384,512]{2,1,0:T(8,128)(2,1)} %refs_2_.1, bf16[6,8,4096]{2,1,0:T(8,128)(2,1)} %bitcast.5, s32[8]{0:T(128)} %refs_4_.1, s32[8,6]{1,0:T(8,128)} %refs_5_.1, s32[2,2,2,3]{3,2,1,0:T(2,128)} %refs_6_.1, ...), custom_call_target="tpu_custom_call" | custom-call | tf_op jit(solution)/shard_map/condense/pallas_call | solution.py:378
  51.7 1.3 %copy.10 = bf16[1,1,24,11,4096]{4,2,3,1,0:T(8,128)(2,1)} copy(bf16[1,1,24,11,4096]{4,2,3,1,0:T(8,128)(2,1)S(1)} %bitcast.4) | data formatting | bytes 4325376

commit v3 on v2

--- a/solution.py
+++ b/solution.py
@@ -65,33 +65,37 @@
         own[e, p] = jnp.where(same_face, moved, 0.0)
 
 
-def pair_of_columns(e, p, orient_ref, to_interior, solved, own, contrib):
+def turned_blocks(e, orient_ref, to_interior, solved, own, place):
     lane = iota((1, LANES), 1)
     second = lane // NFACE
-    codes = jnp.where(second == 1, orient_ref[e, 2 * p + 1], orient_ref[e, 2 * p])
-    target = mapped_nodes(lane % NFACE, codes) + NFACE * second
     wide = iota((2 * LANES, LANES), 0)
-    move = (target == wide % NFACE + NFACE * (wide // LANES)).astype(BF16)
-    columns = solved[e, :, p * LANES : (p + 1) * LANES]
-    blocks = -jnp.dot(to_interior[e], columns, preferred_element_type=F32)
-    parts = [blocks[a * LANES : (a + 1) * LANES] for a in range(3)]
-    parts[p] = parts[p] + own[e, p]
-    blocks = lax.dot_general(
-        jnp.concatenate(parts, axis=0).astype(BF16),
-        move,
-        (((1,), (1,)), ((), ())),
-        preferred_element_type=F32,
-    )
+    wide_node = wide % NFACE + NFACE * (wide // LANES)
     even_lanes = iota((HALF, LANES), 1) < NFACE
-    for a in range(FACES):
-        top = blocks[a * NFACE : a * NFACE + HALF]
-        bottom = blocks[a * NFACE + HALF : (a + 1) * NFACE]
-        for q in range(2):
-            at = slice(q * LANES, (q + 1) * LANES)
-            contrib[e, a, 2 * p + q] = jnp.where(even_lanes, top[:, at], bottom[:, at]).astype(BF16)
-
-
-RUNS = ((0, 1), (1, 2), (3, 2), (5, 6))
+    coupled = jnp.dot(to_interior[e], solved[e], preferred_element_type=F32)
+    for p in range(3):
+        codes = jnp.where(second == 1, orient_ref[e, 2 * p + 1], orient_ref[e, 2 * p])
+        target = mapped_nodes(lane % NFACE, codes) + NFACE * second
+        move = (target == wide_node).astype(BF16)
+        blocks = -coupled[:, p * LANES : (p + 1) * LANES]
+        parts = [blocks[a * LANES : (a + 1) * LANES] for a in range(3)]
+        parts[p] = parts[p] + own[e, p]
+        blocks = lax.dot_general(
+            jnp.concatenate(parts, axis=0).astype(BF16),
+            move,
+            (((1,), (1,)), ((), ())),
+            preferred_element_type=F32,
+        )
+        for a in range(FACES):
+            top = blocks[a * NFACE : a * NFACE + HALF]
+            bottom = blocks[a * NFACE + HALF : (a + 1) * NFACE]
+            for q in range(2):
+                at = slice(q * LANES, (q + 1) * LANES)
+                merged = jnp.where(even_lanes, top[:, at], bottom[:, at])
+                place[a, 2 * p + q] = merged.astype(BF16)
+
+
+RUNS = ((0, 5), (5, 6))
+AHEAD = 2
 
 
 def condense_kernel(
@@ -119,7 +123,6 @@
     diag_rows,
     own,
     contrib,
-    rim,
     right,
     stage,
     landed,
@@ -159,9 +162,13 @@
         source, place = ((inverse_hbm, inverse), (to_face_hbm, to_face), (to_interior_hbm, to_interior))[i]
         return pltpu.make_async_copy(source.at[e], place.at[e], arrive.at[e, i])
 
-    for e in range(E_DEV):
-        for i in range(3):
-            input_of(e, i).start()
+    def fetch(i):
+        for e in (2 * i, 2 * i + 1):
+            for n in range(3):
+                input_of(e, n).start()
+
+    for i in range(AHEAD):
+        fetch(i)
 
     barrier = pltpu.get_barrier_semaphore()
     greeted = [below[0], below[1], above[0], above[1]]
@@ -179,14 +186,6 @@
             found = jnp.where(cell_ref[e] == c, e, found)
         element_ref[c] = found
 
-    @pl.loop(0, F_DEV)
-    def _(v):
-        found = 0
-        for f in range(F_DEV):
-            at = (f // 12, f // 6 % 2, f // 3 % 2, f % 3)
-            found = jnp.where(owner_ref[at] == v, f, found)
-        slot_ref[v] = found
-
     for a in range(FACES):
         faces = diag[a].astype(F32)
         for r in range(HALF):
@@ -199,33 +198,77 @@
         for e in (2 * i, 2 * i + 1):
             for n in range(3):
                 input_of(e, n).wait()
+
+        @pl.when(i + AHEAD < E_DEV // 2)
+        def _():
+            fetch(i + AHEAD)
+
         for e in (2 * i, 2 * i + 1):
             product = jnp.dot(inverse[e], to_face[e], preferred_element_type=F32)
             solved[e] = product.astype(BF16)
             turn_rows(e, orient_ref, to_interior, diag_rows, own)
 
-    def columns(p):
-        @pl.loop(0, E_DEV // 2)
-        def _(i):
-            for e in (2 * i, 2 * i + 1):
-                pair_of_columns(e, p, orient_ref, to_interior, solved, own, contrib)
+        for q in range(F_DEV // (E_DEV // 2)):
+            v = F_DEV // (E_DEV // 2) * i + q
+            found = 0
+            for f in range(F_DEV):
+                at = (f // 12, f // 6 % 2, f // 3 % 2, f % 3)
+                found = jnp.where(owner_ref[at] == v, f, found)
+            slot_ref[v] = found
+
+    def halo(d, i):
+        cy, cz = lax.rem(i, 2), i // 2
+        source, place = (
+            (contrib.at[0, cy, cz, 0], right.at[0, 1, cy, cz]),
+            (contrib.at[:, cy, cz, 2], right.at[1, :, 1, cz]),
+            (contrib.at[:, cy, cz, 4], right.at[2, :, cy, 1]),
+        )[d]
+        return pltpu.make_async_remote_copy(
+            src_ref=source,
+            dst_ref=place,
+            send_sem=halo_send.at[d, i],
+            recv_sem=halo_recv.at[d, i],
+            device_id=below[d],
+            device_id_type=MESH,
+        )
+
+    def each_halo(i, act):
+        @pl.when(lax.rem(i, 2) == 0)
+        def _():
+            act(halo(1, i))
+
+        @pl.when(i // 2 == 0)
+        def _():
+            act(halo(2, i))
+
+        act(halo(0, i))
+
+    pl.semaphore_wait(barrier, len(greeted))
+
+    @pl.loop(0, E_DEV // 2)
+    def _(i):
+        cy, cz = lax.rem(i, 2), i // 2
+        for cx in range(2):
+            e = element_ref[4 * cx + 2 * cy + cz]
+            place = contrib.at[cx, cy, cz]
+            turned_blocks(e, orient_ref, to_interior, solved, own, place)
+        each_halo(i, lambda copy: copy.start())
 
     def face_of(k, j):
         f = slot_ref[PER * lax.rem(gz + k, n_gz) + j]
         cell, d = f // 3, f % 3
         cx, cy, cz = cell // 4, cell // 2 % 2, cell % 2
         keep = 1 - flag_ref[cx, cy, cz, d]
-        return cell, cx, cy, cz, d, keep
+        return cx, cy, cz, d, keep
 
     def stage_left(k, run):
         first, size = RUNS[run]
         for j in range(PER):
-            cell, _, _, _, d, keep = face_of(k, j)
-            e = element_ref[cell]
+            cx, cy, cz, d, keep = face_of(k, j)
             scale = jnp.full((HALF, LANES), keep, jnp.int32).astype(F32).astype(BF16)
             for b in range(first, first + size):
                 other = b + (b >= 2 * d + 1).astype(jnp.int32)
-                stage[k, j, b] = contrib[e, 2 * d + 1, other] * scale
+                stage[k, j, b] = contrib[cx, cy, cz, 2 * d + 1, other] * scale
 
     diagonal = (
         iota((HALF, LANES), 1) % NFACE == 2 * iota((HALF, LANES), 0) + iota((HALF, LANES), 1) // NFACE
@@ -233,11 +276,10 @@
 
     def stage_right(k):
         for j in range(PER):
-            cell, cx, cy, cz, d, keep = face_of(k, j)
-            e = element_ref[cell]
+            cx, cy, cz, d, keep = face_of(k, j)
             wide = jnp.full((HALF, LANES), keep, jnp.int32).astype(F32)
             scale = wide.astype(BF16)
-            total = contrib[e, 2 * d + 1, 2 * d + 1].astype(F32) + right[
+            total = contrib[cx, cy, cz, 2 * d + 1, 2 * d + 1].astype(F32) + right[
                 d, cx, cy, cz, 2 * d
             ].astype(F32)
             stage[k, j, 5] = (total * wide + diagonal * (1.0 - wide)).astype(BF16)
@@ -264,49 +306,24 @@
 
         stage_left(0, run)
 
-    columns(0)
-    pl.semaphore_wait(barrier, len(greeted))
     send_left(0)
-    columns(1)
-    send_left(1)
-    columns(2)
-
-    for d in range(3):
-        step = (4, 2, 1)[d]
-        free = ((2, 1), (4, 1), (4, 2))[d]
-
+
+    @pl.loop(0, 2)
+    def _(u):
         @pl.loop(0, 2)
-        def _(u):
-            @pl.loop(0, 2)
-            def _(w):
-                cell = free[0] * u + free[1] * w
-                rim[d, u, w] = contrib[element_ref[cell], 2 * d]
-                at = ((0, u, w), (u, 0, w), (u, w, 0))[d]
-                right[(d, *at)] = contrib[element_ref[cell + step], 2 * d]
-
-    halo = []
-    for d in range(3):
-        place = (right.at[0, 1], right.at[1, :, 1], right.at[2, :, :, 1])[d]
-        copy = pltpu.make_async_remote_copy(
-            src_ref=rim.at[d],
-            dst_ref=place,
-            send_sem=halo_send.at[d],
-            recv_sem=halo_recv.at[d],
-            device_id=below[d],
-            device_id_type=MESH,
-        )
-        copy.start()
-        halo.append(copy)
-
-    send_left(2)
-
-    for copy in halo:
-        copy.wait_recv()
+        def _(w):
+            right[0, 0, u, w] = contrib[1, u, w, 0]
+            right[1, u, 0, w] = contrib[u, 1, w, 2]
+            right[2, u, w, 0] = contrib[u, w, 1, 4]
+
+    @pl.loop(0, E_DEV // 2)
+    def _(i):
+        each_halo(i, lambda copy: copy.wait_recv())
 
     @pl.loop(1, n_gz)
     def _(k):
         stage_right(k)
-        push(k, 3).start()
+        push(k, 1).start()
 
     stage_right(0)
 
@@ -320,42 +337,49 @@
                 at = pl.multiple_of((start + j) * rows_at + to * HALF, HALF)
                 flat[pl.ds(at, HALF), :] = source[k, j, b].astype(F32)
 
-    def unfold(b):
+    def unfold(b, first, count):
         for r in range(HALF):
-            out_ref[b, :, r * LANES : (r + 1) * LANES] = flat[
-                pl.ds(b * HALF + r, F_DEV, stride=rows_at), :
+            out_ref[b, pl.ds(first, count), r * LANES : (r + 1) * LANES] = flat[
+                pl.ds(first * rows_at + b * HALF + r, count, stride=rows_at), :
             ].astype(BF16)
 
     spread(stage, 0, 0, 11)
 
     @pl.loop(1, n_gz)
     def _(k):
-        for run in range(3):
-            push(k, run).wait_recv()
+        push(k, 0).wait_recv()
         spread(landed, k, 0, 5)
 
     @pl.loop(1, 6)
     def _(b):
-        unfold(b)
+        unfold(b, 0, F_DEV)
+
+    done = 0
+    for source in range(n_gz):
+        k = lax.rem(gz - source + n_gz, n_gz)
+
+        @pl.when(k != 0)
+        def _():
+            push(k, 1).wait_recv()
+            spread(landed, k, 5, 6)
+
+        ready = (source + 1) * PER // 8 * 8
+        if ready > done:
+
+            @pl.loop(5, 11)
+            def _(b, done=done, ready=ready):
+                unfold(jnp.where(b == 5, 0, b), done, ready - done)
+
+            done = ready
 
     @pl.loop(1, n_gz)
     def _(k):
-        push(k, 3).wait_recv()
-        spread(landed, k, 5, 6)
-
-    unfold(0)
-
-    @pl.loop(6, 11)
-    def _(b):
-        unfold(b)
-
-    @pl.loop(1, n_gz)
-    def _(k):
-        for run in range(4):
+        for run in range(2):
             push(k, run).wait_send()
 
-    for copy in halo:
-        copy.wait_send()
+    @pl.loop(0, E_DEV // 2)
+    def _(i):
+        each_halo(i, lambda copy: copy.wait_send())
 
 
 def shards(
@@ -394,18 +418,17 @@
             pltpu.VMEM((E_DEV, NINT, WIDTH), BF16),
             pltpu.VMEM((E_DEV * FACES * HALF, LANES), F32),
             pltpu.VMEM((E_DEV, 3, LANES, LANES), F32),
-            pltpu.VMEM((E_DEV, FACES, FACES, *block), BF16),
-            pltpu.VMEM((3, 2, 2, FACES, *block), BF16),
+            pltpu.VMEM((2, 2, 2, FACES, FACES, *block), BF16),
             pltpu.VMEM((3, 2, 2, 2, FACES, *block), BF16),
             pltpu.VMEM((n_gz, PER, 11, *block), BF16),
             pltpu.VMEM((n_gz, PER, 11, *block), BF16),
             pltpu.VMEM((F_DEV * 11 * HALF, LANES), F32),
             pltpu.SemaphoreType.DMA((E_DEV, 3)),
             pltpu.SemaphoreType.DMA((5,)),
-            pltpu.SemaphoreType.DMA((3,)),
-            pltpu.SemaphoreType.DMA((3,)),
-            pltpu.SemaphoreType.DMA((n_gz, 4)),
-            pltpu.SemaphoreType.DMA((n_gz, 4)),
+            pltpu.SemaphoreType.DMA((3, E_DEV // 2)),
+            pltpu.SemaphoreType.DMA((3, E_DEV // 2)),
+            pltpu.SemaphoreType.DMA((n_gz, 2)),
+            pltpu.SemaphoreType.DMA((n_gz, 2)),
         ],
         compiler_params=pltpu.CompilerParams(
             collective_id=0, has_side_effects=True, vmem_limit_bytes=40 << 20

time: 53.1 us -> 48 us (0.904)
  Pallas kernels: 51.7 us -> 46.5 us
    pallas_call x1, Pallas kernels: 51.7 us -> 46.5 us  [shards(): pl.pallas_call(body, out_shape=jax.ShapeDtypeStruct((11, F_DEV, NFACE * N...]
where the time goes in v3:
time: 48 us; the launch traced here: 47.9 us
  Pallas kernels  46.5 us (97%)
  local copies, waits for them, and re-layouts  1.34 us (3%)
    pallas_call x1, Pallas kernels, shards(): pl.pallas_call(body, out_shape=jax.ShapeDtypeStruct((11, F_DEV, NFACE * N...  46.5 us
    unnamed x1, local copies, waits for them, and re-layouts  1.34 us

profile of v3, /device:TPU:70, one launch (start us, length us, event | category | flops | bytes accessed | tf_op | source)
XLA Modules:
  0.0 47.9 jit_solution(18255317249328235829)
XLA Ops:
  0.0 46.5 %condense.1 = bf16[11,24,4096]{2,1,0:T(8,128)(2,1)S(1)} custom-call(bf16[8,512,512]{2,1,0:T(8,128)(2,1)} %refs_0_.1, bf16[8,512,384]{2,1,0:T(8,128)(2,1)} %refs_1_.1, bf16[8,384,512]{2,1,0:T(8,128)(2,1)} %refs_2_.1, bf16[6,8,4096]{2,1,0:T(8,128)(2,1)} %bitcast.5, s32[8]{0:T(128)} %refs_4_.1, s32[8,6]{1,0:T(8,128)} %refs_5_.1, s32[2,2,2,3]{3,2,1,0:T(2,128)} %refs_6_.1, ...), custom_call_target="tpu_custom_call" | custom-call | tf_op jit(solution)/shard_map/condense/pallas_call | solution.py:402
  46.6 1.3 %copy.10 = bf16[1,1,24,11,4096]{4,2,3,1,0:T(8,128)(2,1)} copy(bf16[1,1,24,11,4096]{4,2,3,1,0:T(8,128)(2,1)S(1)} %bitcast.4) | data formatting | bytes 4325376

commit v4 on v3

--- a/solution.py
+++ b/solution.py
@@ -95,6 +95,7 @@
 
 
 RUNS = ((0, 5), (5, 6))
+CELLS_AT = 32
 AHEAD = 2
 
 
@@ -117,8 +118,8 @@
     orient_ref,
     owner_ref,
     flag_ref,
-    element_ref,
-    slot_ref,
+    table_ref,
+    table,
     solved,
     diag_rows,
     own,
@@ -133,6 +134,7 @@
     halo_recv,
     send,
     recv,
+    table_sem,
 ):
     n_gx, n_gy, n_gz = counts
     gx, gy, gz = lax.axis_index("gx"), lax.axis_index("gy"), lax.axis_index("gz")
@@ -179,12 +181,16 @@
     for copy in small:
         copy.wait()
 
-    @pl.loop(0, E_DEV)
-    def _(c):
-        found = 0
-        for e in range(E_DEV):
-            found = jnp.where(cell_ref[e] == c, e, found)
-        element_ref[c] = found
+    at = iota((1, LANES), 1)
+    found = jnp.zeros((1, LANES), jnp.int32)
+    for f in range(F_DEV):
+        owner = owner_ref[f // 12, f // 6 % 2, f // 3 % 2, f % 3]
+        found = jnp.where(at == owner, f, found)
+    for e in range(E_DEV):
+        found = jnp.where(at == CELLS_AT + cell_ref[e], e, found)
+    table[...] = found
+    table_copy = pltpu.make_async_copy(table, table_ref, table_sem)
+    table_copy.start()
 
     for a in range(FACES):
         faces = diag[a].astype(F32)
@@ -208,13 +214,7 @@
             solved[e] = product.astype(BF16)
             turn_rows(e, orient_ref, to_interior, diag_rows, own)
 
-        for q in range(F_DEV // (E_DEV // 2)):
-            v = F_DEV // (E_DEV // 2) * i + q
-            found = 0
-            for f in range(F_DEV):
-                at = (f // 12, f // 6 % 2, f // 3 % 2, f % 3)
-                found = jnp.where(owner_ref[at] == v, f, found)
-            slot_ref[v] = found
+    table_copy.wait()
 
     def halo(d, i):
         cy, cz = lax.rem(i, 2), i // 2
@@ -233,15 +233,16 @@
         )
 
     def each_halo(i, act):
+        @pl.when(i // 2 == 0)
+        def _():
+            act(halo(2, i))
+
         @pl.when(lax.rem(i, 2) == 0)
         def _():
             act(halo(1, i))
 
-        @pl.when(i // 2 == 0)
-        def _():
-            act(halo(2, i))
-
         act(halo(0, i))
+
 
     pl.semaphore_wait(barrier, len(greeted))
 
@@ -249,13 +250,13 @@
     def _(i):
         cy, cz = lax.rem(i, 2), i // 2
         for cx in range(2):
-            e = element_ref[4 * cx + 2 * cy + cz]
+            e = table_ref[0, CELLS_AT + 4 * cx + 2 * cy + cz]
             place = contrib.at[cx, cy, cz]
             turned_blocks(e, orient_ref, to_interior, solved, own, place)
         each_halo(i, lambda copy: copy.start())
 
     def face_of(k, j):
-        f = slot_ref[PER * lax.rem(gz + k, n_gz) + j]
+        f = table_ref[0, PER * lax.rem(gz + k, n_gz) + j]
         cell, d = f // 3, f % 3
         cx, cy, cz = cell // 4, cell // 2 % 2, cell % 2
         keep = 1 - flag_ref[cx, cy, cz, d]
@@ -300,7 +301,8 @@
 
     def send_left(run):
         @pl.loop(1, n_gz)
-        def _(k):
+        def _(q):
+            k = jnp.where(lax.rem(gz, 2) == 1, n_gz - q, q)
             stage_left(k, run)
             push(k, run).start()
 
@@ -321,7 +323,8 @@
         each_halo(i, lambda copy: copy.wait_recv())
 
     @pl.loop(1, n_gz)
-    def _(k):
+    def _(q):
+        k = jnp.where(lax.rem(gz, 2) == 1, n_gz - q, q)
         stage_right(k)
         push(k, 1).start()
 
@@ -413,8 +416,8 @@
             pltpu.SMEM((E_DEV, FACES), jnp.int32),
             pltpu.SMEM((2, 2, 2, 3), jnp.int32),
             pltpu.SMEM((2, 2, 2, 3), jnp.int32),
-            pltpu.SMEM((E_DEV,), jnp.int32),
-            pltpu.SMEM((F_DEV,), jnp.int32),
+            pltpu.SMEM((1, LANES), jnp.int32),
+            pltpu.VMEM((1, LANES), jnp.int32),
             pltpu.VMEM((E_DEV, NINT, WIDTH), BF16),
             pltpu.VMEM((E_DEV * FACES * HALF, LANES), F32),
             pltpu.VMEM((E_DEV, 3, LANES, LANES), F32),
@@ -429,6 +432,7 @@
             pltpu.SemaphoreType.DMA((3, E_DEV // 2)),
             pltpu.SemaphoreType.DMA((n_gz, 2)),
             pltpu.SemaphoreType.DMA((n_gz, 2)),
+            pltpu.SemaphoreType.DMA,
         ],
         compiler_params=pltpu.CompilerParams(
             collective_id=0, has_side_effects=True, vmem_limit_bytes=40 << 20

time: 48 us -> 45.8 us (0.954)
  Pallas kernels: 46.5 us -> 44.4 us
    pallas_call x1, Pallas kernels: 46.5 us -> 44.4 us  [shards(): pl.pallas_call(body, out_shape=jax.ShapeDtypeStruct((11, F_DEV, NFACE * N...]
where the time goes in v4:
time: 45.8 us; the launch traced here: 45.7 us
  Pallas kernels  44.4 us (97%)
  local copies, waits for them, and re-layouts  1.34 us (3%)
    pallas_call x1, Pallas kernels, shards(): pl.pallas_call(body, out_shape=jax.ShapeDtypeStruct((11, F_DEV, NFACE * N...  44.4 us
    unnamed x1, local copies, waits for them, and re-layouts  1.34 us

profile of v4, /device:TPU:70, one launch (start us, length us, event | category | flops | bytes accessed | tf_op | source)
XLA Modules:
  0.0 45.7 jit_solution(1917752725213000786)
XLA Ops:
  0.0 44.4 %condense.1 = bf16[11,24,4096]{2,1,0:T(8,128)(2,1)S(1)} custom-call(bf16[8,512,512]{2,1,0:T(8,128)(2,1)} %refs_0_.1, bf16[8,512,384]{2,1,0:T(8,128)(2,1)} %refs_1_.1, bf16[8,384,512]{2,1,0:T(8,128)(2,1)} %refs_2_.1, bf16[6,8,4096]{2,1,0:T(8,128)(2,1)} %bitcast.5, s32[8]{0:T(128)} %refs_4_.1, s32[8,6]{1,0:T(8,128)} %refs_5_.1, s32[2,2,2,3]{3,2,1,0:T(2,128)} %refs_6_.1, ...), custom_call_target="tpu_custom_call" | custom-call | tf_op jit(solution)/shard_map/condense/pallas_call | solution.py:405
  44.4 1.3 %copy.10 = bf16[1,1,24,11,4096]{4,2,3,1,0:T(8,128)(2,1)} copy(bf16[1,1,24,11,4096]{4,2,3,1,0:T(8,128)(2,1)S(1)} %bitcast.4) | data formatting | bytes 4325376

commit v5 on v4

--- a/solution.py
+++ b/solution.py
@@ -71,7 +71,9 @@
     wide = iota((2 * LANES, LANES), 0)
     wide_node = wide % NFACE + NFACE * (wide // LANES)
     even_lanes = iota((HALF, LANES), 1) < NFACE
-    coupled = jnp.dot(to_interior[e], solved[e], preferred_element_type=F32)
+    coupled = lax.dot_general(
+        to_interior[e], solved[e], (((1,), (1,)), ((), ())), preferred_element_type=F32
+    )
     for p in range(3):
         codes = jnp.where(second == 1, orient_ref[e, 2 * p + 1], orient_ref[e, 2 * p])
         target = mapped_nodes(lane % NFACE, codes) + NFACE * second
@@ -169,8 +171,7 @@
             for n in range(3):
                 input_of(e, n).start()
 
-    for i in range(AHEAD):
-        fetch(i)
+    fetch(0)
 
     barrier = pltpu.get_barrier_semaphore()
     greeted = [below[0], below[1], above[0], above[1]]
@@ -199,6 +200,9 @@
                 :, r * LANES : (r + 1) * LANES
             ]
 
+    for i in range(1, AHEAD):
+        fetch(i)
+
     @pl.loop(0, E_DEV // 2)
     def _(i):
         for e in (2 * i, 2 * i + 1):
@@ -210,7 +214,9 @@
             fetch(i + AHEAD)
 
         for e in (2 * i, 2 * i + 1):
-            product = jnp.dot(inverse[e], to_face[e], preferred_element_type=F32)
+            product = lax.dot_general(
+                to_face[e], inverse[e], (((0,), (1,)), ((), ())), preferred_element_type=F32
+            )
             solved[e] = product.astype(BF16)
             turn_rows(e, orient_ref, to_interior, diag_rows, own)
 
@@ -418,7 +424,7 @@
             pltpu.SMEM((2, 2, 2, 3), jnp.int32),
             pltpu.SMEM((1, LANES), jnp.int32),
             pltpu.VMEM((1, LANES), jnp.int32),
-            pltpu.VMEM((E_DEV, NINT, WIDTH), BF16),
+            pltpu.VMEM((E_DEV, WIDTH, NINT), BF16),
             pltpu.VMEM((E_DEV * FACES * HALF, LANES), F32),
             pltpu.VMEM((E_DEV, 3, LANES, LANES), F32),
             pltpu.VMEM((2, 2, 2, FACES, FACES, *block), BF16),

time: 45.8 us -> 45 us (0.983)
  Pallas kernels: 44.4 us -> 43.5 us
    pallas_call x1, Pallas kernels: 44.4 us -> 43.5 us  [shards(): pl.pallas_call(body, out_shape=jax.ShapeDtypeStruct((11, F_DEV, NFACE * N...]
where the time goes in v5:
time: 45 us; the launch traced here: 44.9 us
  Pallas kernels  43.5 us (97%)
  local copies, waits for them, and re-layouts  1.34 us (3%)
    pallas_call x1, Pallas kernels, shards(): pl.pallas_call(body, out_shape=jax.ShapeDtypeStruct((11, F_DEV, NFACE * N...  43.5 us
    unnamed x1, local copies, waits for them, and re-layouts  1.34 us

profile of v5, /device:TPU:70, one launch (start us, length us, event | category | flops | bytes accessed | tf_op | source)
XLA Modules:
  0.0 44.9 jit_solution(9251269486404053275)
XLA Ops:
  0.0 43.5 %condense.1 = bf16[11,24,4096]{2,1,0:T(8,128)(2,1)S(1)} custom-call(bf16[8,512,512]{2,1,0:T(8,128)(2,1)} %refs_0_.1, bf16[8,512,384]{2,1,0:T(8,128)(2,1)} %refs_1_.1, bf16[8,384,512]{2,1,0:T(8,128)(2,1)} %refs_2_.1, bf16[6,8,4096]{2,1,0:T(8,128)(2,1)} %bitcast.5, s32[8]{0:T(128)} %refs_4_.1, s32[8,6]{1,0:T(8,128)} %refs_5_.1, s32[2,2,2,3]{3,2,1,0:T(2,128)} %refs_6_.1, ...), custom_call_target="tpu_custom_call" | custom-call | tf_op jit(solution)/shard_map/condense/pallas_call | solution.py:411
  43.5 1.3 %copy.10 = bf16[1,1,24,11,4096]{4,2,3,1,0:T(8,128)(2,1)} copy(bf16[1,1,24,11,4096]{4,2,3,1,0:T(8,128)(2,1)S(1)} %bitcast.4) | data formatting | bytes 4325376
